TPU v7x, 32 devices: a whole 2x2x4 slice. The times are simulated.
32 devices in a mesh: row: 8 (over y, x, core), col: 4 (over z).
Axes of the slice: x: 2, y: 2, z: 4, core: 2. Of those that a mesh axis runs over, the one named last changes fastest.
Arguments:
- legendre: bfloat16 [4, 128, 89, 8, 128], P(None, 'col', None, 'row'), may hold values from -6 to 6
- longitude: float32 [512], replicated, may hold values from -3.140625 to 3.140625
- obs_weight: float32 [512], replicated, may hold values from 0.1 to 1.9
- span_weight: float32 [8], replicated, may hold values from 0.3 to 3
- span_of: int32 [512], replicated, may hold values from 0 to 7
- tile_order: int32 [712], replicated, may hold values from 0 to 711, each once
- slab_start: int32 [1], replicated, may hold values from 0 to 704
- resident: float32 [89, 8, 4, 128, 128], P(None, 'row', 'col'), may hold values from -6 to 6
Outputs:
- updated: float32 [89, 8, 4, 128, 128], P(None, 'row', 'col')
Inputs may be any that keep to these rules, and one draw needn't show every extreme that they name: tile_order is a permutation of the slot positions.
All inputs are finite; a program needn't handle non-finite values.
Results may differ from a plain program's by a relative error of at most 0.00074.
Values may be sent and summed in bfloat16 or wider, within the bound.
No kernel may reach another device: no remote copies, remote signals or barrier semaphores. Data moves between devices by JAX's collectives and lax.ppermute only.
A program may use at most 64 MiB of HBM per device.

v0:
```python
import math
import jax
import jax.numpy as jnp
from jax import lax
from jax.sharding import PartitionSpec as P

DEGREE = 300
UNK = 90600


def lookup_weights(obs_weight, span_weight, span_of):
    group_count = span_weight.shape[0]
    matches = span_of[:, None] == jnp.arange(group_count, dtype=jnp.int32)[None, :]
    factor = jnp.sum(jnp.where(matches, span_weight[None, :], 0.0), axis=1)
    return obs_weight * factor * (0.25 / math.sqrt(obs_weight.shape[0]))


def locate(tile_order, targets):
    places = jnp.arange(tile_order.shape[0], dtype=jnp.int32)
    return jnp.sum(jnp.where(tile_order[None, :] == targets[:, None], places[None, :], 0), axis=1)


def contract_rows(left_side, right_side):
    return lax.dot_general(
        left_side, right_side, (((0,), (0,)), ((), ())), preferred_element_type=jnp.float32
    )


def per_device(
    legendre, longitude, obs_weight, span_weight, span_of, tile_order, slab_start, resident
):
    block_count, shard_rows, slot_count, _, tile_size = legendre.shape
    row_count = lax.axis_size("row")
    col_count = lax.axis_size("col")
    row_index = lax.axis_index("row")
    col_index = lax.axis_index("col")
    block_rows = shard_rows * col_count
    order_map = tile_order.reshape(slot_count, row_count)
    own_tiles = lax.dynamic_slice_in_dim(order_map, row_index, 1, 1)[:, 0]
    unknown = own_tiles[:, None] * tile_size + jnp.arange(tile_size, dtype=jnp.int32)[None, :]
    orders = (unknown % (DEGREE + 1)).astype(jnp.float32).reshape(1, slot_count * tile_size)
    is_valid = (unknown < UNK).reshape(1, slot_count * tile_size)
    targets = slab_start[0] + jnp.arange(col_count, dtype=jnp.int32)
    positions = locate(tile_order, targets)
    target = targets[col_index]
    root_row = positions[col_index] % row_count
    root_slots = positions // row_count
    root_slot = root_slots[col_index]
    is_root = row_index == root_row
    weights = lookup_weights(obs_weight, span_weight, span_of).reshape(block_count, block_rows)
    angles = longitude.reshape(block_count, block_rows)
    in_lower = own_tiles >= target
    zero_piece = jnp.zeros((), jnp.bfloat16)
    all_values = legendre.reshape(block_count * shard_rows, slot_count * tile_size)
    own_angles = lax.dynamic_slice_in_dim(angles, col_index * shard_rows, shard_rows, 1)
    own_angles = own_angles.reshape(block_count * shard_rows)
    design_all = jnp.where(
        is_valid, all_values.astype(jnp.float32) * jnp.cos(own_angles[:, None] * orders), 0.0
    ).astype(jnp.bfloat16)
    design_all = design_all.reshape(block_count, shard_rows, slot_count * tile_size)
    gathered = lax.all_gather(design_all, "col", axis=1, tiled=True)
    gathered = gathered.reshape(block_count * block_rows, slot_count * tile_size)
    candidate = lax.dynamic_slice_in_dim(gathered, root_slot * tile_size, tile_size, 1)
    column = lax.psum(jnp.where(is_root, candidate, zero_piece), "row").astype(jnp.float32)
    weighted = (weights.reshape(block_count * block_rows)[:, None] * column).astype(jnp.bfloat16)
    running = contract_rows(gathered, weighted)
    update = jnp.where(
        in_lower[:, None, None], running.reshape(slot_count, tile_size, tile_size), 0.0
    )
    return resident + update.reshape(resident.shape)


def solution(mesh):
    placed = (
        P(None, "col", None, "row", None),
        P(),
        P(),
        P(),
        P(),
        P(),
        P(),
        P(None, "row", "col", None, None),
    )
    return jax.shard_map(
        per_device,
        mesh=mesh,
        in_specs=placed,
        out_specs=P(None, "row", "col", None, None),
        check_vma=False,
    )
```

profile of v0, /device:TPU:0, one launch (start us, length us, event | category | flops | bytes accessed | tf_op | source)
XLA Modules:
  0.0 322.1 jit_solution(3542823524447298766)
XLA Ops:
  6.5 0.0 copy-start
  6.5 0.0 all-gather.2.cloned.1.call-start
  6.5 0.8 reshape.90
  7.3 0.2 multiply_reduce_fusion
  7.5 0.1 fusion.4
  7.6 0.1 fusion.8
  7.7 5.5 %copy.20 = f32[4,32,89,1,128]{4,2,1,0,3:T(8,128)} copy(bf16[4,32,89,1,128]{4,1,3,2,0:T(8,128)(2,1)} %param.8) | data formatting | bytes 8749056 | tf_op jit(solution)/shard_map/convert_element_type | solution.py:58
  13.2 7.2 %reshape.94 = f32[4,32,11392]{2,1,0:T(8,128)} reshape(f32[4,32,89,1,128]{4,2,1,0,3:T(8,128)} %copy.20) | data formatting | bytes 11665408 | tf_op jit(solution)/shard_map/convert_element_type | solution.py:58
  20.4 0.0 copy-done
  20.4 0.1 constant_dynamic-slice_fusion
  20.5 0.0 copy-start.1
  20.5 0.0 copy-start.3
  20.5 0.0 copy-start.4
  20.5 0.0 copy-start.2
  20.5 22.0 %select_convert_fusion = bf16[4,32,11392]{2,1,0:T(8,128)(2,1)} fusion(f32[4,32,11392]{2,1,0:T(8,128)} %reshape.94, f32[11392]{0:T(1024)S(1)} %fusion.4, f32[4,32]{1,0:T(4,128)S(1)} %constant_dynamic-slice_fusion, pred[11392]{0:T(1024)(128)(4,1)S(1)} %fusion.8), kind=kLoop, calls=%fused_computation.2 | loop fusion | flops 5832704 | bytes 8806528 | tf_op jit(solution)/shard_map/convert_element_type | solution.py:59
  42.6 0.0 all-gather.2.cloned.1.call-update
  42.6 0.0 all-reduce.2.cloned.1.call-start
  43.3 0.0 copy-done.1
  43.3 0.2 select_reduce_fusion.1
  43.5 0.6 dynamic_slice.21
  46.0 0.6 dynamic_slice.22
  47.3 0.0 copy-done.3
  47.3 0.0 copy-done.4
  47.3 0.1 select_reduce_fusion
  47.4 201.2 %all-gather.2.cloned.1.call-done = bf16[4,128,11392]{2,1,0:T(8,128)(2,1)} async-done(((bf16[4,32,11392]{2,1,0:T(8,128)(2,1)}), bf16[4,128,11392]{2,1,0:T(8,128)(2,1)}) %all-gather.2.cloned.1.call-update) | async-done | bytes 11665424 | tf_op jit(solution)/shard_map/all_gather | solution.py:61
  248.6 1.6 dynamic-slice_select_fusion
  250.2 0.0 all-reduce.2.cloned.1.call-update
  250.3 0.0 copy-done.2
  250.3 0.6 dynamic_slice.19
  250.9 0.8 compare_reduce_fusion
  251.7 16.2 %copy.21 = bf16[11392,512]{1,0:T(8,128)(2,1)} copy(bf16[11392,512]{0,1:T(8,128)(2,1)} %bitcast.39) | data formatting | bytes 23330816 | tf_op jit(solution)/shard_map/dot_general | solution.py:24
  267.9 35.4 %all-reduce.2.cloned.1.call-done = bf16[512,128]{1,0:T(8,128)(2,1)} async-done(((bf16[512,128]{1,0:T(8,128)(2,1)}), bf16[512,128]{1,0:T(8,128)(2,1)}) %all-reduce.2.cloned.1.call-update) | async-done | bytes 131088 | tf_op jit(solution)/shard_map/psum | solution.py:64
  303.3 11.9 %fusion = f32[89,1,1,128,128]{4,3,2,1,0:T(8,128)} fusion(f32[89,1,1,128,128]{4,3,2,1,0:T(8,128)} %param.15, pred[89]{0:T(512)(128)(4,1)S(1)} %compare_reduce_fusion, bf16[89,128,512]{2,1,0:T(8,128)(2,1)} %bitcast.37, bf16[512,128]{1,0:T(8,128)(2,1)} %all-reduce.2.cloned.1.call-done, f32[512]{0:T(512)S(1)} %multiply_multiply_fusion), kind=kOutput, calls=%fused_computation.1 | convolution fusion | flops 1496285184 | bytes 23464024 | tf_op jit(solution)/shard_map/dot_general | solution.py:24
  (3 shorter events, 0.0 us)
Async XLA Ops:
  6.5 13.9 %copy-start = (f32[512]{0:T(512)S(1)}, f32[512]{0:T(512)}, u32[]{:S(2)}) copy-start(f32[512]{0:T(512)} %param.9) | copy-start | bytes 6148
  6.5 242.1 %all-gather.2.cloned.1.call-start = ((), (), s32[]{:S(2)}) async-start(), calls=%async_computation | async-start | bytes 14581760 | tf_op jit(solution)/shard_map/all_gather | solution.py:61
  20.5 22.8 %copy-start.1 = (s32[712]{0:T(1024)S(1)}, s32[712]{0:T(1024)}, u32[]{:S(2)}) copy-start(s32[712]{0:T(1024)} %param.13) | copy-start | bytes 8548
  20.5 26.8 %copy-start.3 = (s32[512]{0:T(512)S(1)}, s32[512]{0:T(512)}, u32[]{:S(2)}) copy-start(s32[512]{0:T(512)} %param.12) | copy-start | bytes 6148
  20.5 26.8 %copy-start.4 = (f32[8]{0:T(128)S(1)}, f32[8]{0:T(128)}, u32[]{:S(2)}) copy-start(f32[8]{0:T(128)} %param.11) | copy-start | bytes 100
  20.5 229.8 %copy-start.2 = (f32[512]{0:T(512)S(1)}, f32[512]{0:T(512)}, u32[]{:S(2)}) copy-start(f32[512]{0:T(512)} %param.10) | copy-start | bytes 6148
  42.6 260.7 %all-reduce.2.cloned.1.call-start = ((), (), s32[]{:S(2)}) async-start(), calls=%async_computation.1 | async-start | bytes 262144 | tf_op jit(solution)/shard_map/psum | solution.py:64
Sparse Core Ops, SparseCore 0:
  42.7 205.8 all-gather.1
  251.7 51.6 all-reduce.1
where the time goes:
time: 323 us; the launch traced here: 322 us
  waiting for transfers between devices  237 us (73%)
  local copies, waits for them, and re-layouts  31.5 us (10%)
  other arithmetic  25.1 us (8%)
  between operations  16.8 us (5%)
  matrix products  11.9 us (4%)
    all_gather x1, waiting for transfers between devices, per_device(): gathered = lax.all_gather(design_all, 'col', axis=1, tiled=True)  201 us
    psum x1, waiting for transfers between devices, per_device(): lax.psum(jnp.where(is_root, candidate, zero_piece), 'row')  35.4 us
    convert_element_type x1, other arithmetic, per_device(): design_all = jnp.where(is_valid, all_values.astype(jnp.float32) * jnp.cos...  22 us
    dot_general x1, local copies, waits for them, and re-layouts, contract_rows(): lax.dot_general(left_side, right_side, (((0,), (0,)), ((), ())), preferre...  16.2 us
    convert_element_type x2, local copies, waits for them, and re-layouts, per_device(): all_values.astype(jnp.float32) * jnp.cos(own_angles[:, None] * orders)  12.7 us
    dot_general x1, matrix products, contract_rows(): lax.dot_general(left_side, right_side, (((0,), (0,)), ((), ())), preferre...  11.9 us
  transfers between devices with their start and end apart: 2, of which 2 were waited for; matrix products, arithmetic and copies ran while one was open for 6% of the time, Pallas kernels for 0%

commit v1 on v0

--- a/solution.py
+++ b/solution.py
@@ -61,7 +61,9 @@
     gathered = lax.all_gather(design_all, "col", axis=1, tiled=True)
     gathered = gathered.reshape(block_count * block_rows, slot_count * tile_size)
     candidate = lax.dynamic_slice_in_dim(gathered, root_slot * tile_size, tile_size, 1)
-    column = lax.psum(jnp.where(is_root, candidate, zero_piece), "row").astype(jnp.float32)
+    column = jnp.sum(
+        lax.all_gather(jnp.where(is_root, candidate, zero_piece), "row"), axis=0
+    ).astype(jnp.float32)
     weighted = (weights.reshape(block_count * block_rows)[:, None] * column).astype(jnp.bfloat16)
     running = contract_rows(gathered, weighted)
     update = jnp.where(

time: 323 us -> 293 us (0.907)
  waiting for transfers between devices: 237 us -> 206 us
    psum x1 -> x0, waiting for transfers between devices: 35.4 us -> none  [per_device(): lax.psum(jnp.where(is_root, candidate, zero_piece), 'row')]
    dot_general x1 -> x0, local copies, waits for them, and re-layouts: 16.2 us -> none  [contract_rows(): lax.dot_general(left_side, right_side, (((0,), (0,)), ((), ())), preferre...]
    reshape x0 -> x1, local copies, waits for them, and re-layouts: none -> 16.2 us  [per_device(): gathered.reshape(block_count * block_rows, slot_count * tile_size)]
    all_gather x0 -> x1, waiting for transfers between devices: none -> 4.16 us  [per_device(): lax.all_gather(jnp.where(is_root, candidate, zero_piece), 'row')]
  transfers between devices with their start and end apart: 2 -> 2, of which waited for: 2 -> 2; matrix products, arithmetic and copies ran while one was open for 6% -> 7% of each run, Pallas kernels for 0% -> 0%
where the time goes in v1:
time: 293 us; the launch traced here: 292 us
  waiting for transfers between devices  206 us (70%)
  local copies, waits for them, and re-layouts  31.5 us (11%)
  other arithmetic  26.5 us (9%)
  between operations  16.8 us (6%)
  matrix products  11.8 us (4%)
    all_gather x1, waiting for transfers between devices, per_device(): gathered = lax.all_gather(design_all, 'col', axis=1, tiled=True)  201 us
    convert_element_type x1, other arithmetic, per_device(): design_all = jnp.where(is_valid, all_values.astype(jnp.float32) * jnp.cos...  22 us
    reshape x1, local copies, waits for them, and re-layouts, per_device(): gathered.reshape(block_count * block_rows, slot_count * tile_size)  16.2 us
    convert_element_type x2, local copies, waits for them, and re-layouts, per_device(): all_values.astype(jnp.float32) * jnp.cos(own_angles[:, None] * orders)  12.7 us
    dot_general x1, matrix products, contract_rows(): lax.dot_general(left_side, right_side, (((0,), (0,)), ((), ())), preferre...  11.8 us
  transfers between devices with their start and end apart: 2, of which 2 were waited for; matrix products, arithmetic and copies ran while one was open for 7% of the time, Pallas kernels for 0%

profile of v1, /device:TPU:0, one launch (start us, length us, event | category | flops | bytes accessed | tf_op | source)
XLA Modules:
  0.0 292.2 jit_solution(13314810340058614182)
XLA Ops:
  6.5 0.0 copy-start
  6.5 0.0 all-gather.4.cloned.1.call-start
  6.5 0.8 reshape.90
  7.3 0.2 multiply_reduce_fusion
  7.5 0.1 fusion.4
  7.6 0.1 fusion.8
  7.7 5.5 %copy.19 = f32[4,32,89,1,128]{4,2,1,0,3:T(8,128)} copy(bf16[4,32,89,1,128]{4,1,3,2,0:T(8,128)(2,1)} %param.8) | data formatting | bytes 8749056 | tf_op jit(solution)/shard_map/convert_element_type | solution.py:58
  13.2 7.2 %reshape.94 = f32[4,32,11392]{2,1,0:T(8,128)} reshape(f32[4,32,89,1,128]{4,2,1,0,3:T(8,128)} %copy.19) | data formatting | bytes 11665408 | tf_op jit(solution)/shard_map/convert_element_type | solution.py:58
  20.4 0.0 copy-done
  20.4 0.1 constant_dynamic-slice_fusion
  20.5 0.0 copy-start.1
  20.5 0.0 copy-start.3
  20.5 0.0 copy-start.4
  20.5 0.0 copy-start.2
  20.5 22.0 %select_convert_fusion = bf16[4,32,11392]{2,1,0:T(8,128)(2,1)} fusion(f32[4,32,11392]{2,1,0:T(8,128)} %reshape.94, f32[11392]{0:T(1024)S(1)} %fusion.4, f32[4,32]{1,0:T(4,128)S(1)} %constant_dynamic-slice_fusion, pred[11392]{0:T(1024)(128)(4,1)S(1)} %fusion.8), kind=kLoop, calls=%fused_computation.2 | loop fusion | flops 5832704 | bytes 8806528 | tf_op jit(solution)/shard_map/convert_element_type | solution.py:59
  42.6 0.0 all-gather.4.cloned.1.call-update
  42.6 0.0 all-gather.6.cloned.1.call-start
  43.3 0.0 copy-done.1
  43.3 0.2 select_reduce_fusion.1
  43.5 0.6 dynamic_slice.21
  46.0 0.6 dynamic_slice.22
  47.3 201.3 %all-gather.4.cloned.1.call-done = bf16[4,128,11392]{2,1,0:T(8,128)(2,1)} async-done(((bf16[4,32,11392]{2,1,0:T(8,128)(2,1)}), bf16[4,128,11392]{2,1,0:T(8,128)(2,1)}) %all-gather.4.cloned.1.call-update) | async-done | bytes 11665424 | tf_op jit(solution)/shard_map/all_gather | solution.py:61
  248.6 1.6 dynamic-slice_select_fusion
  250.2 0.0 all-gather.6.cloned.1.call-update
  250.3 0.6 dynamic_slice.19
  250.9 0.8 compare_reduce_fusion
  251.7 0.0 copy-done.3
  251.7 0.0 copy-done.4
  251.7 0.1 select_reduce_fusion
  251.8 0.0 copy-done.2
  251.8 16.2 %copy.20 = bf16[512,11392]{0,1:T(8,128)(2,1)} copy(bf16[512,11392]{1,0:T(8,128)(2,1)} %bitcast.40) | data formatting | bytes 23330816 | tf_op jit(solution)/shard_map/reshape | solution.py:62
  268.0 4.2 %all-gather.6.cloned.1.call-done = bf16[4096,128]{1,0:T(8,128)(2,1)} async-done(((bf16[512,128]{1,0:T(8,128)(2,1)}), bf16[4096,128]{1,0:T(8,128)(2,1)}) %all-gather.6.cloned.1.call-update) | async-done | bytes 1048592 | tf_op jit(solution)/shard_map/all_gather | solution.py:65
  272.1 1.4 reduce_sum.32
  273.5 11.8 %fusion = f32[89,1,1,128,128]{4,3,2,1,0:T(8,128)} fusion(f32[89,1,1,128,128]{4,3,2,1,0:T(8,128)} %param.15, pred[89]{0:T(512)(128)(4,1)S(1)} %compare_reduce_fusion, bf16[89,128,512]{2,1,0:T(8,128)(2,1)} %bitcast.38, bf16[512,128]{1,0:T(8,128)(2,1)S(1)} %reduce_sum.32, f32[512]{0:T(512)S(1)} %multiply_multiply_fusion), kind=kOutput, calls=%fused_computation.1 | convolution fusion | flops 1496285184 | bytes 23464024 | tf_op jit(solution)/shard_map/dot_general | solution.py:24
  (3 shorter events, 0.0 us)
Async XLA Ops:
  6.5 13.9 %copy-start = (f32[512]{0:T(512)S(1)}, f32[512]{0:T(512)}, u32[]{:S(2)}) copy-start(f32[512]{0:T(512)} %param.9) | copy-start | bytes 6148
  6.5 242.1 %all-gather.4.cloned.1.call-start = ((), (), s32[]{:S(2)}) async-start(), calls=%async_computation | async-start | bytes 14581760 | tf_op jit(solution)/shard_map/all_gather | solution.py:61
  20.5 22.8 %copy-start.1 = (s32[712]{0:T(1024)S(1)}, s32[712]{0:T(1024)}, u32[]{:S(2)}) copy-start(s32[712]{0:T(1024)} %param.13) | copy-start | bytes 8548
  20.5 231.2 %copy-start.3 = (s32[512]{0:T(512)S(1)}, s32[512]{0:T(512)}, u32[]{:S(2)}) copy-start(s32[512]{0:T(512)} %param.12) | copy-start | bytes 6148
  20.5 231.2 %copy-start.4 = (f32[8]{0:T(128)S(1)}, f32[8]{0:T(128)}, u32[]{:S(2)}) copy-start(f32[8]{0:T(128)} %param.11) | copy-start | bytes 100
  20.5 231.3 %copy-start.2 = (f32[512]{0:T(512)S(1)}, f32[512]{0:T(512)}, u32[]{:S(2)}) copy-start(f32[512]{0:T(512)} %param.10) | copy-start | bytes 6148
  42.6 229.5 %all-gather.6.cloned.1.call-start = ((), (), s32[]{:S(2)}) async-start(), calls=%async_computation.1 | async-start | bytes 1179648 | tf_op jit(solution)/shard_map/all_gather | solution.py:65
Sparse Core Ops, SparseCore 0:
  42.7 205.8 all-gather.3
  250.5 21.5 all-gather.5
